TPU v7x, 128 devices: a whole 4x4x4 slice. The times are simulated.
128 devices in a mesh: pts: 32 (over z, x, core), rep: 4 (over y).
Axes of the slice: x: 4, y: 4, z: 4, core: 2. Of those that a mesh axis runs over, the one named last changes fastest.
Arguments:
- target_xyz: float32 [3, 32768], P(None, 'pts'), may hold values from 0 to 1
- source_xyz: float32 [3, 65536], P(None, ('pts', 'rep')), may hold values from 0 to 1
- target_count: int32 [32], P('pts'), may hold values from 1 to 1024, as said below
- source_count: int32 [128], P(('pts', 'rep')), may hold values from 1 to 512, as said below
- psi: bfloat16 [32768, 256], P('pts'), may hold values from -6 to 6
- omega: bfloat16 [65536, 256], P(('pts', 'rep')), may hold values from -6 to 6
Outputs:
- range_sketch: float32 [32768, 256], P('pts')
- corange_sketch: float32 [65536, 256], P(('pts', 'rep'))
- core: float32 [256, 256], replicated
- range_gram: float32 [256, 256], replicated
- corange_gram: float32 [256, 256], replicated
Inputs may be any that keep to these rules, and one draw needn't show every extreme that they name: `target_count`: each group holds 1 to 1024 live targets; some group holds exactly 1024. `source_count`: each shard holds 1 to 512 live sources; some shard holds exactly 512.
All inputs are finite; a program needn't handle non-finite values.
Results may differ from a plain program's by a relative error of at most 0.0003.
The roundings to bfloat16 on the way count: a program that leaves them out, or rounds other values in their place, can miss the bound.
Values may be sent and summed in bfloat16 or wider, within the bound.
No kernel may reach another device: no remote copies, remote signals or barrier semaphores. Data moves between devices by JAX's collectives and lax.ppermute only.
A program may use at most 64 MiB of HBM per device.

v0:
```python
import math
import jax
import jax.numpy as jnp
from jax import lax
from jax.sharding import PartitionSpec as P

SHIFT = 1.05
SPREAD = 8.0


def tile_block(tgt, src):
    dx = tgt[0][:, None] - (src[0][None, :] + SHIFT)
    dy = SPREAD * (tgt[1][:, None] - src[1][None, :])
    dz = SPREAD * (tgt[2][:, None] - src[2][None, :])
    return lax.rsqrt(dx * dx + dy * dy + dz * dz).astype(jnp.bfloat16)


def local(target_xyz, source_xyz, target_count, source_count, psi, omega):
    tcap = psi.shape[0]
    scap = omega.shape[0]
    width = psi.shape[1]
    n_pts = lax.axis_size("pts")
    n_rep = lax.axis_size("rep")
    all_targets = tcap * n_pts
    all_sources = scap * n_pts * n_rep
    tlive = jnp.arange(tcap, dtype=jnp.int32) < target_count[0]
    slive = jnp.arange(scap, dtype=jnp.int32) < source_count[0]
    psi_live = jnp.where(tlive[:, None], psi, jnp.zeros_like(psi))
    omega_live = jnp.where(slive[:, None], omega, jnp.zeros_like(omega))
    hi = lax.Precision.HIGHEST
    src_all = lax.all_gather(source_xyz, "pts", axis=1, tiled=True)
    piece = lax.all_gather(omega_live, "pts", axis=0, tiled=True)

    def range_inner(j, acc):
        rows = lax.dynamic_slice_in_dim(piece, j * scap, scap, 0)
        where = lax.dynamic_slice_in_dim(src_all, j * scap, scap, 1)
        return acc + jnp.dot(
            tile_block(target_xyz, where), rows, preferred_element_type=jnp.float32
        )

    y_part = lax.fori_loop(
        0, piece.shape[0] // scap, range_inner, jnp.zeros((tcap, width), jnp.float32)
    )
    y_sum = lax.psum(y_part, "rep") * (2.0 / math.sqrt(all_sources))
    range_sketch = jnp.where(tlive[:, None], y_sum, jnp.zeros_like(y_sum))
    tgt_all = lax.all_gather(target_xyz, "pts", axis=1, tiled=True)
    corange_piece = lax.all_gather(psi_live, "pts", axis=0, tiled=True)

    def corange_inner(j, acc):
        rows = lax.dynamic_slice_in_dim(corange_piece, j * tcap, tcap, 0)
        where = lax.dynamic_slice_in_dim(tgt_all, j * tcap, tcap, 1)
        tile = tile_block(where, source_xyz)
        return acc + lax.dot_general(
            tile, rows, (((0,), (0,)), ((), ())), preferred_element_type=jnp.float32
        )

    z_sum = lax.fori_loop(
        0, corange_piece.shape[0] // tcap, corange_inner, jnp.zeros((scap, width), jnp.float32)
    )
    z_scaled = z_sum * (2.0 / math.sqrt(all_targets))
    corange_sketch = jnp.where(slive[:, None], z_scaled, jnp.zeros_like(z_scaled))
    z_gram_part = jnp.dot(corange_sketch.T, corange_sketch, precision=hi)
    core_part = jnp.dot(psi_live.astype(jnp.float32).T, range_sketch, precision=hi)
    y_gram_part = jnp.dot(range_sketch.T, range_sketch, precision=hi)
    core_sum, y_gram = lax.psum((core_part, y_gram_part), "pts")
    z_gram = lax.psum(z_gram_part, ("pts", "rep"))
    core = core_sum / math.sqrt(all_targets)
    range_gram = y_gram / all_targets
    corange_gram = z_gram / all_sources
    return (range_sketch, corange_sketch, core, range_gram, corange_gram)


def solution(mesh):
    return jax.shard_map(
        local,
        mesh=mesh,
        in_specs=(
            P(None, "pts"),
            P(None, ("pts", "rep")),
            P("pts"),
            P(("pts", "rep")),
            P("pts", None),
            P(("pts", "rep"), None),
        ),
        out_specs=(P("pts", None), P(("pts", "rep"), None), P(), P(), P()),
        check_vma=False,
    )
```

profile of v0, /device:TPU:1, one launch (start us, length us, event | category | flops | bytes accessed | tf_op | source)
XLA Modules:
  0.0 550.0 jit_solution(14603858195827019406)
XLA Ops:
  9.7 27.6 %all_gather.12 = f32[3,16384]{1,0:T(4,128)S(1)} all-gather(f32[3,512]{1,0:T(4,128)} %param.11), channel_id=1, replica_groups=mesh['pts'=32,'rep'=4] {'pts'}, dimensions={1}, use_global_device_ids=true | all-gather | bytes 202752 | tf_op jit(solution)/shard_map/all_gather | solution.py:31
  37.3 30.2 %all-gather.3.cloned.1.call-done = bf16[16384,256]{1,0:T(8,128)(2,1)} async-done(((bf16[512,256]{1,0:T(8,128)(2,1)}), bf16[16384,256]{1,0:T(8,128)(2,1)}) %all-gather.3.cloned.1.call-update) | async-done | bytes 8388624 | tf_op jit(solution)/shard_map/all_gather | solution.py:32
  67.5 96.4 %while.28 = (s32[]{:T(128)}, f32[1024,256]{1,0:T(8,128)S(1)}, f32[3,1024]{1,0:T(4,128)}, f32[3,16384]{1,0:T(4,128)S(1)}, bf16[16384,256]{1,0:T(8,128)(2,1)}, /*i...) while((s32[]{:T(128)}, f32[1024,256]{1,0:T(8,128)S(1)}, ...), condition=%wide.region_1.2_spmd.clone, body=%wide.region_0.1_spmd.clone.sunk | while | flops 274727424 | bytes 2414797 | solution.py:41
  166.7 24.7 %all_gather.14 = f32[3,32768]{1,0:T(4,128)S(1)} all-gather(f32[3,1024]{1,0:T(4,128)S(1)} %copy-done.5), channel_id=1, replica_groups=mesh['pts'=32,'rep'=4] {'pts'}, dimensions={1}, use_global_device_ids=true | all-gather | bytes 405504 | tf_op jit(solution)/shard_map/all_gather | solution.py:46
  191.4 17.0 %all-reduce.5.cloned.1.call-done = f32[1024,256]{1,0:T(8,128)} async-done(((f32[1024,256]{1,0:T(8,128)}), f32[1024,256]{1,0:T(8,128)}) %all-reduce.5.cloned.1.call-update) | async-done | bytes 1048592 | tf_op jit(solution)/shard_map/psum | solution.py:44
  211.4 2.6 fusion.22
  214.0 73.1 %all-gather.5.cloned.1.call-done = bf16[32768,256]{1,0:T(8,128)(2,1)} async-done(((bf16[1024,256]{1,0:T(8,128)(2,1)}), bf16[32768,256]{1,0:T(8,128)(2,1)}) %all-gather.5.cloned.1.call-update) | async-done | bytes 16777232 | tf_op jit(solution)/shard_map/all_gather | solution.py:47
  287.1 81.4 %while.29 = (s32[]{:T(128)}, f32[512,256]{1,0:T(8,128)S(1)}, f32[3,32768]{1,0:T(4,128)S(1)}, f32[3,512]{1,0:T(4,128)S(1)}, bf16[32768,256]{1,0:T(8,128)(2,1)}, /...) while((s32[]{:T(128)}, f32[512,256]{1,0:T(8,128)S(1)}, ...), condition=%wide.region_4.5_spmd.clone, body=%wide.region_3.4_spmd.clone.sunk | while | flops 274465280 | bytes 1628365 | solution.py:57
  287.2 2.4 convolution_add_fusion.5
  289.8 2.4 convolution_add_fusion.5
  292.3 2.4 convolution_add_fusion.5
  294.8 2.4 convolution_add_fusion.5
  297.4 2.4 convolution_add_fusion.5
  300.0 2.4 convolution_add_fusion.5
  302.5 2.4 convolution_add_fusion.5
  305.0 2.4 convolution_add_fusion.5
  315.2 2.4 convolution_add_fusion.5
  317.8 2.4 convolution_add_fusion.5
  320.3 2.4 convolution_add_fusion.5
  322.9 2.4 convolution_add_fusion.5
  325.4 2.4 convolution_add_fusion.5
  327.9 2.4 convolution_add_fusion.5
  333.0 2.4 convolution_add_fusion.5
  335.6 2.4 convolution_add_fusion.5
  338.1 2.4 convolution_add_fusion.5
  348.3 2.4 convolution_add_fusion.5
  350.9 2.4 convolution_add_fusion.5
  355.9 2.4 convolution_add_fusion.5
  358.5 2.4 convolution_add_fusion.5
  361.0 2.4 convolution_add_fusion.5
  370.5 24.1 %all-reduce.9.cloned.1.call-done = (f32[256,256]{1,0:T(8,128)}, f32[256,256]{1,0:T(8,128)}) async-done(((f32[256,256]{1,0:T(8,128)}, f32[256,256]{1,0:T(8,128)}), (f32[256,256]{1,0:T(8,128)}, f32[256,256]{1,0:T(8,128)})) %all-reduce.9.cloned.1.call-update) | async-done | bytes 524304 | tf_op jit(solution)/shard_map/psum | solution.py:65
  396.4 145.4 %all-reduce.7.cloned.1.call-done = f32[256,256]{1,0:T(8,128)} async-done(((f32[256,256]{1,0:T(8,128)}), f32[256,256]{1,0:T(8,128)}) %all-reduce.7.cloned.1.call-update) | async-done | bytes 262160 | tf_op jit(solution)/shard_map/psum | solution.py:66
  (206 shorter events, 134.8 us)
Async XLA Ops:
  7.2 60.3 %all-gather.3.cloned.1.call-start = ((), (), s32[]{:S(2)}) async-start(), calls=%async_computation | async-start | bytes 8650752 | tf_op jit(solution)/shard_map/all_gather | solution.py:32
  9.7 198.7 %all-reduce.5.cloned.1.call-start = ((), (), s32[]{:S(2)}) async-start(), calls=%async_computation.1 | async-start | bytes 2097152 | tf_op jit(solution)/shard_map/psum | solution.py:44
  67.5 98.1 %copy-start.4 = (bf16[1024,256]{1,0:T(8,128)(2,1)S(1)}, bf16[1024,256]{1,0:T(8,128)(2,1)}, u32[]{:S(2)}) copy-start(bf16[1024,256]{1,0:T(8,128)(2,1)} %param.14) | copy-start | bytes 1572868
  163.9 1.0 copy-start.3
  163.9 2.8 copy-start.5
  164.9 122.2 %all-gather.5.cloned.1.call-start = ((), (), s32[]{:S(2)}) async-start(), calls=%async_computation.2 | async-start | bytes 17301504 | tf_op jit(solution)/shard_map/all_gather | solution.py:47
  166.6 43.2 %copy-start.2 = (bf16[1024,256]{1,0:T(8,128)(2,1)S(1)}, bf16[1024,256]{1,0:T(8,128)(2,1)}, u32[]{:S(2)}) copy-start(bf16[1024,256]{1,0:T(8,128)(2,1)} %broadcast_select_fusion) | copy-start | bytes 1572868
  166.6 227.9 %all-reduce.9.cloned.1.call-start = ((), (), s32[]{:S(2)}) async-start(), calls=%async_computation.4 | async-start | bytes 1048576 | tf_op jit(solution)/shard_map/psum | solution.py:65
  209.8 4.1 copy-start
  209.9 77.3 %copy-start.6 = (f32[3,512]{1,0:T(4,128)S(1)}, f32[3,512]{1,0:T(4,128)}, u32[]{:S(2)}) copy-start(f32[3,512]{1,0:T(4,128)} %param.11) | copy-start | bytes 18436
  214.0 327.8 %all-reduce.7.cloned.1.call-start = ((), (), s32[]{:S(2)}) async-start(), calls=%async_computation.3 | async-start | bytes 524288 | tf_op jit(solution)/shard_map/psum | solution.py:66
  368.7 174.8 %copy-start.1 = (f32[512,256]{1,0:T(8,128)}, f32[512,256]{1,0:T(8,128)S(1)}, u32[]{:S(2)}) copy-start(f32[512,256]{1,0:T(8,128)S(1)} %multiply_select_fusion.1) | copy-start | bytes 1572868
Sparse Core Ops, SparseCore 0:
  10.8 56.6 all-gather.2
  165.0 43.3 all-reduce.4
  211.2 75.8 all-gather.4
  290.8 103.6 all-reduce.8
  399.1 142.5 all-reduce.6
where the time goes:
time: 555 us; the launch traced here: 550 us
  waiting for transfers between devices  290 us (52%)
  matrix products  148 us (27%)
  blocking collectives  52.2 us (9%)
  local copies, waits for them, and re-layouts  30.9 us (6%)
  between operations  15.2 us (3%)
  other arithmetic  10.8 us (2%)
    psum x1, waiting for transfers between devices, local(): z_gram = lax.psum(z_gram_part, ('pts', 'rep'))  145 us
    dot_general x32, matrix products, corange_inner(): lax.dot_general(tile, rows, (((0,), (0,)), ((), ())), preferred_element_t...  76.9 us
    all_gather x1, waiting for transfers between devices, local(): corange_piece = lax.all_gather(psi_live, 'pts', axis=0, tiled=True)  73.1 us
    dot_general x32, matrix products, range_inner(): jnp.dot(tile_block(target_xyz, where), rows, preferred_element_type=jnp.f...  65.5 us
    all_gather x1, waiting for transfers between devices, local(): piece = lax.all_gather(omega_live, 'pts', axis=0, tiled=True)  30.2 us
    slice x64, local copies, waits for them, and re-layouts, tile_block(): dx = tgt[0][:, None] - (src[0][None, :] + SHIFT)  30 us
    all_gather x1, blocking collectives, local(): src_all = lax.all_gather(source_xyz, 'pts', axis=1, tiled=True)  27.6 us
    all_gather x1, blocking collectives, local(): tgt_all = lax.all_gather(target_xyz, 'pts', axis=1, tiled=True)  24.7 us
  transfers between devices with their start and end apart: 5, of which 5 were waited for; matrix products, arithmetic and copies ran while one was open for 16% of the time, Pallas kernels for 0%

commit v1 on v0

--- a/solution.py
+++ b/solution.py
@@ -6,6 +6,11 @@
 
 SHIFT = 1.05
 SPREAD = 8.0
+
+
+def by_each_axis(value, inner_axis, outer_axis):
+    half = lax.psum(value, inner_axis)
+    return lax.psum(half, outer_axis)
 
 
 def tile_block(tgt, src):
@@ -63,7 +68,7 @@
     core_part = jnp.dot(psi_live.astype(jnp.float32).T, range_sketch, precision=hi)
     y_gram_part = jnp.dot(range_sketch.T, range_sketch, precision=hi)
     core_sum, y_gram = lax.psum((core_part, y_gram_part), "pts")
-    z_gram = lax.psum(z_gram_part, ("pts", "rep"))
+    z_gram = by_each_axis(z_gram_part, "pts", "rep")
     core = core_sum / math.sqrt(all_targets)
     range_gram = y_gram / all_targets
     corange_gram = z_gram / all_sources

time: 555 us -> 530 us (0.955)
  waiting for transfers between devices: 290 us -> 264 us
    psum x1, waiting for transfers between devices: 145 us -> 39.7 us  [by_each_axis(): return lax.psum(half, outer_axis)]
    psum x1, waiting for transfers between devices: 24.1 us -> 104 us  [local(): core_sum, y_gram = lax.psum((core_part, y_gram_part), 'pts')]
  transfers between devices with their start and end apart: 5 -> 5, of which waited for: 5 -> 5; matrix products, arithmetic and copies ran while one was open for 16% -> 2% of each run, Pallas kernels for 0% -> 0%
where the time goes in v1:
time: 530 us; the launch traced here: 524 us
  waiting for transfers between devices  264 us (50%)
  matrix products  148 us (28%)
  blocking collectives  52.2 us (10%)
  local copies, waits for them, and re-layouts  30.9 us (6%)
  between operations  15.2 us (3%)
  other arithmetic  10.8 us (2%)
    psum x1, waiting for transfers between devices, local(): core_sum, y_gram = lax.psum((core_part, y_gram_part), 'pts')  104 us
    dot_general x32, matrix products, corange_inner(): lax.dot_general(tile, rows, (((0,), (0,)), ((), ())), preferred_element_t...  77 us
    all_gather x1, waiting for transfers between devices, local(): corange_piece = lax.all_gather(psi_live, 'pts', axis=0, tiled=True)  73.1 us
    dot_general x32, matrix products, range_inner(): jnp.dot(tile_block(target_xyz, where), rows, preferred_element_type=jnp.f...  65.5 us
    psum x1, waiting for transfers between devices, by_each_axis(): return lax.psum(half, outer_axis)  39.7 us
    all_gather x1, waiting for transfers between devices, local(): piece = lax.all_gather(omega_live, 'pts', axis=0, tiled=True)  30.2 us
    slice x64, local copies, waits for them, and re-layouts, tile_block(): dx = tgt[0][:, None] - (src[0][None, :] + SHIFT)  29.9 us
    all_gather x1, blocking collectives, local(): src_all = lax.all_gather(source_xyz, 'pts', axis=1, tiled=True)  27.6 us
  transfers between devices with their start and end apart: 5, of which 5 were waited for; matrix products, arithmetic and copies ran while one was open for 2% of the time, Pallas kernels for 0%

profile of v1, /device:TPU:1, one launch (start us, length us, event | category | flops | bytes accessed | tf_op | source)
XLA Modules:
  0.0 523.9 jit_solution(3442788399810201816)
XLA Ops:
  9.7 27.6 %all_gather.12 = f32[3,16384]{1,0:T(4,128)S(1)} all-gather(f32[3,512]{1,0:T(4,128)} %param.11), channel_id=1, replica_groups=mesh['pts'=32,'rep'=4] {'pts'}, dimensions={1}, use_global_device_ids=true | all-gather | bytes 202752 | tf_op jit(solution)/shard_map/all_gather | solution.py:36
  37.3 30.2 %all-gather.3.cloned.1.call-done = bf16[16384,256]{1,0:T(8,128)(2,1)} async-done(((bf16[512,256]{1,0:T(8,128)(2,1)}), bf16[16384,256]{1,0:T(8,128)(2,1)}) %all-gather.3.cloned.1.call-update) | async-done | bytes 8388624 | tf_op jit(solution)/shard_map/all_gather | solution.py:37
  67.5 96.4 %while.28 = (s32[]{:T(128)}, f32[1024,256]{1,0:T(8,128)S(1)}, f32[3,1024]{1,0:T(4,128)}, f32[3,16384]{1,0:T(4,128)S(1)}, bf16[16384,256]{1,0:T(8,128)(2,1)}, /*i...) while((s32[]{:T(128)}, f32[1024,256]{1,0:T(8,128)S(1)}, ...), condition=%wide.region_1.2_spmd.clone, body=%wide.region_0.1_spmd.clone.sunk | while | flops 274727424 | bytes 2414797 | solution.py:46
  166.7 24.7 %all_gather.14 = f32[3,32768]{1,0:T(4,128)S(1)} all-gather(f32[3,1024]{1,0:T(4,128)S(1)} %copy-done.5), channel_id=1, replica_groups=mesh['pts'=32,'rep'=4] {'pts'}, dimensions={1}, use_global_device_ids=true | all-gather | bytes 405504 | tf_op jit(solution)/shard_map/all_gather | solution.py:51
  191.4 17.0 %all-reduce.5.cloned.1.call-done = f32[1024,256]{1,0:T(8,128)} async-done(((f32[1024,256]{1,0:T(8,128)}), f32[1024,256]{1,0:T(8,128)}) %all-reduce.5.cloned.1.call-update) | async-done | bytes 1048592 | tf_op jit(solution)/shard_map/psum | solution.py:49
  211.4 2.6 fusion.22
  214.0 73.1 %all-gather.5.cloned.1.call-done = bf16[32768,256]{1,0:T(8,128)(2,1)} async-done(((bf16[1024,256]{1,0:T(8,128)(2,1)}), bf16[32768,256]{1,0:T(8,128)(2,1)}) %all-gather.5.cloned.1.call-update) | async-done | bytes 16777232 | tf_op jit(solution)/shard_map/all_gather | solution.py:52
  287.1 81.4 %while.29 = (s32[]{:T(128)}, f32[512,256]{1,0:T(8,128)S(1)}, f32[3,32768]{1,0:T(4,128)S(1)}, f32[3,512]{1,0:T(4,128)S(1)}, bf16[32768,256]{1,0:T(8,128)(2,1)}, /...) while((s32[]{:T(128)}, f32[512,256]{1,0:T(8,128)S(1)}, ...), condition=%wide.region_4.5_spmd.clone, body=%wide.region_3.4_spmd.clone.sunk | while | flops 274465280 | bytes 1628365 | solution.py:62
  287.2 2.4 convolution_add_fusion.5
  289.8 2.4 convolution_add_fusion.5
  292.3 2.4 convolution_add_fusion.5
  294.8 2.4 convolution_add_fusion.5
  299.9 2.4 convolution_add_fusion.5
  305.0 2.4 convolution_add_fusion.5
  310.1 2.4 convolution_add_fusion.5
  312.6 2.4 convolution_add_fusion.5
  315.2 2.4 convolution_add_fusion.5
  317.7 2.4 convolution_add_fusion.5
  320.3 2.4 convolution_add_fusion.5
  325.4 2.4 convolution_add_fusion.5
  330.4 2.4 convolution_add_fusion.5
  333.0 2.4 convolution_add_fusion.5
  335.5 2.4 convolution_add_fusion.5
  338.1 2.4 convolution_add_fusion.5
  340.6 2.4 convolution_add_fusion.5
  345.7 2.4 convolution_add_fusion.5
  350.8 2.4 convolution_add_fusion.5
  355.9 2.4 convolution_add_fusion.5
  361.0 2.4 convolution_add_fusion.5
  366.0 2.4 convolution_add_fusion.5
  370.5 103.7 %all-reduce.9.cloned.1.call-done = (f32[256,256]{1,0:T(8,128)}, f32[256,256]{1,0:T(8,128)}, f32[256,256]{1,0:T(8,128)}) async-done(((f32[256,256]{1,0:T(8,128)}, f32[256,256]{1,0:T(8,128)}, f32[256,256]{1,0:T(8,128)}), (f32[256,256]{1,0:T(8,128)}, f32[256,256]{1,0:T(8,128)}, f32[256,256]{1,0:T(8,128)})) %all-reduce.9.cloned.1.call-update) | async-done | bytes 786448 | tf_op jit(solution)/shard_map/psum | solution.py:70
  476.0 39.7 %all-reduce.7.cloned.1.call-done = f32[256,256]{1,0:T(8,128)} async-done(((f32[256,256]{1,0:T(8,128)}), f32[256,256]{1,0:T(8,128)}) %all-reduce.7.cloned.1.call-update) | async-done | bytes 262160 | tf_op jit(solution)/shard_map/psum | solution.py:13
  (206 shorter events, 134.8 us)
Async XLA Ops:
  7.2 60.3 %all-gather.3.cloned.1.call-start = ((), (), s32[]{:S(2)}) async-start(), calls=%async_computation | async-start | bytes 8650752 | tf_op jit(solution)/shard_map/all_gather | solution.py:37
  9.7 198.7 %all-reduce.5.cloned.1.call-start = ((), (), s32[]{:S(2)}) async-start(), calls=%async_computation.1 | async-start | bytes 2097152 | tf_op jit(solution)/shard_map/psum | solution.py:49
  67.5 98.1 %copy-start.4 = (bf16[1024,256]{1,0:T(8,128)(2,1)S(1)}, bf16[1024,256]{1,0:T(8,128)(2,1)}, u32[]{:S(2)}) copy-start(bf16[1024,256]{1,0:T(8,128)(2,1)} %param.14) | copy-start | bytes 1572868
  163.9 1.0 copy-start.3
  163.9 2.8 copy-start.5
  164.9 122.2 %all-gather.5.cloned.1.call-start = ((), (), s32[]{:S(2)}) async-start(), calls=%async_computation.2 | async-start | bytes 17301504 | tf_op jit(solution)/shard_map/all_gather | solution.py:52
  166.6 43.2 %copy-start.2 = (bf16[1024,256]{1,0:T(8,128)(2,1)S(1)}, bf16[1024,256]{1,0:T(8,128)(2,1)}, u32[]{:S(2)}) copy-start(bf16[1024,256]{1,0:T(8,128)(2,1)} %broadcast_select_fusion) | copy-start | bytes 1572868
  166.6 307.5 %all-reduce.9.cloned.1.call-start = ((), (), s32[]{:S(2)}) async-start(), calls=%async_computation.4 | async-start | bytes 1572864 | tf_op jit(solution)/shard_map/psum | solution.py:70
  209.8 4.1 copy-start
  209.9 77.3 %copy-start.6 = (f32[3,512]{1,0:T(4,128)S(1)}, f32[3,512]{1,0:T(4,128)}, u32[]{:S(2)}) copy-start(f32[3,512]{1,0:T(4,128)} %param.11) | copy-start | bytes 18436
  368.6 148.8 %copy-start.1 = (f32[512,256]{1,0:T(8,128)}, f32[512,256]{1,0:T(8,128)S(1)}, u32[]{:S(2)}) copy-start(f32[512,256]{1,0:T(8,128)S(1)} %multiply_select_fusion.1) | copy-start | bytes 1572868
  370.4 145.3 %all-reduce.7.cloned.1.call-start = ((), (), s32[]{:S(2)}) async-start(), calls=%async_computation.3 | async-start | bytes 524288 | tf_op jit(solution)/shard_map/psum | solution.py:13
Sparse Core Ops, SparseCore 0:
  10.8 56.6 all-gather.2
  165.0 43.3 all-reduce.4
  211.2 75.8 all-gather.4
  370.5 103.5 all-reduce.8
  476.3 39.4 all-reduce.6
